TPU v7x, 32 devices: a whole 2x2x4 slice. The times are simulated.
32 devices in a mesh: row: 4 (over y, x), col: 8 (over z, core).
Axes of the slice: x: 2, y: 2, z: 4, core: 2. Of those that a mesh axis runs over, the one named last changes fastest.
Arguments:
- inv_sep: bfloat16 [24576, 24576], P('row', 'col'), may hold values from -6 to 6
- lower_one: bfloat16 [24576, 256], P('col', 'row'), may hold values from -0.078125 to 0.078125
- upper_one: bfloat16 [256, 24576], P('col', 'row'), may hold values from -0.078125 to 0.078125
- diag_inv_one: float32 [256, 256], replicated, may hold values from -6 to 6
- blocks_one: int32 [40], replicated, may hold values from 0 to 191, as said below
- lower_two: bfloat16 [24576, 256], P('col', 'row'), may hold values from -0.09375 to 0.09375
- upper_two: bfloat16 [256, 24576], P('col', 'row'), may hold values from -0.09375 to 0.09375
- corner_lower: bfloat16 [256, 256], replicated, may hold values from -0.375 to 0.375
- corner_upper: bfloat16 [256, 256], replicated, may hold values from -0.375 to 0.375
- diag_inv_two: float32 [256, 256], replicated, may hold values from -6 to 6
- blocks_two: int32 [32], replicated, may hold values from 0 to 191, as said below
Outputs:
- inv_lower_one: bfloat16 [5120, 256], P(('row', 'col'))
- inv_upper_one: bfloat16 [256, 5120], P('row', 'col')
- inv_diag_one: float32 [256, 256], replicated
- inv_lower_two: bfloat16 [4096, 256], P(('row', 'col'))
- inv_upper_two: bfloat16 [256, 4096], P('row', 'col')
- inv_diag_two: float32 [256, 256], replicated
Inputs may be any that keep to these rules, and one draw needn't show every extreme that they name: `blocks_one`: distinct block indices in increasing order; each aligned run of 24 blocks holds exactly 5 of them; the first and the last block of the separator are listed. `blocks_two`: distinct block indices in increasing order, each of them also in blocks_one; each aligned run of 24 blocks holds exactly 4 of them; the first and the last block of the separator are listed.
All inputs are finite; a program needn't handle non-finite values.
Results may differ from a plain program's by a relative error of at most 0.0039.
Values may be sent and summed in bfloat16 or wider, within the bound.
No kernel may reach another device: no remote copies, remote signals or barrier semaphores. Data moves between devices by JAX's collectives and lax.ppermute only.
A program may use at most 128 MiB of HBM per device.

v0:
```python
import jax
import jax.numpy as jnp
from jax import lax
from jax.sharding import PartitionSpec as P

B = 128


def highest(first_mat, second_mat):
    return jnp.dot(
        first_mat.astype(jnp.float32),
        second_mat.astype(jnp.float32),
        precision=lax.Precision.HIGHEST,
    )


def take_rows(matrix, blocks):
    shaped = matrix.reshape(matrix.shape[0] // B, B, matrix.shape[1])
    return jnp.take(shaped, blocks, axis=0).reshape(blocks.shape[0] * B, matrix.shape[1])


def take_cols(matrix, blocks):
    shaped = matrix.reshape(matrix.shape[0], matrix.shape[1] // B, B)
    return jnp.take(shaped, blocks, axis=1).reshape(matrix.shape[0], blocks.shape[0] * B)


def block_rows(blocks):
    return (blocks[:, None] * B + jnp.arange(B, dtype=jnp.int32)[None, :]).reshape(-1)


def places(wanted, listed):
    return jnp.sum((listed[None, :] < wanted[:, None]).astype(jnp.int32), axis=1)


def on_device(
    inv_sep,
    lower_one,
    upper_one,
    diag_inv_one,
    blocks_one,
    lower_two,
    upper_two,
    corner_lower,
    corner_upper,
    diag_inv_two,
    blocks_two,
):
    row_index = lax.axis_index("row")
    col_index = lax.axis_index("col")
    row_count = lax.axis_size("row")
    col_count = lax.axis_size("col")
    rows_here, cols_here = inv_sep.shape
    panel_width = diag_inv_one.shape[0]
    run_blocks = cols_here // B
    pick_one = blocks_one.shape[0] // col_count
    pick_two = blocks_two.shape[0] // col_count
    runs_group = col_count // row_count
    group_one = pick_one * runs_group
    group_two = pick_two * runs_group
    share_one = pick_one * B // row_count
    share_two = pick_two * B // row_count
    upper_rows = panel_width // row_count
    row_one = lax.dynamic_slice_in_dim(blocks_one, row_index * group_one, group_one) - row_index * (
        rows_here // B
    )
    row_two = lax.dynamic_slice_in_dim(blocks_two, row_index * group_two, group_two) - row_index * (
        rows_here // B
    )
    col_one = (
        lax.dynamic_slice_in_dim(blocks_one, col_index * pick_one, pick_one)
        - col_index * run_blocks
    )
    col_two = (
        lax.dynamic_slice_in_dim(blocks_two, col_index * pick_two, pick_two)
        - col_index * run_blocks
    )
    sep_one = take_cols(take_rows(inv_sep, row_one), col_one)
    sep_two = take_cols(take_rows(inv_sep, row_two), col_two)
    lower_spots = block_rows(places(row_two, row_one))
    upper_spots = places(col_two, col_one)
    corner_mine = lax.dynamic_slice_in_dim(corner_upper, row_index * upper_rows, upper_rows, 1)
    lower_p = lax.all_gather(take_rows(lower_one, col_one), "row", axis=1, tiled=True)
    upper_p = lax.all_gather(take_cols(upper_one, row_one), "col", axis=0, tiled=True)
    inv_lower_one = lax.psum_scatter(
        -jnp.dot(sep_one, lower_p, preferred_element_type=jnp.float32),
        "col",
        scatter_dimension=0,
        tiled=True,
    ).astype(jnp.bfloat16)
    inv_upper_one = lax.psum_scatter(
        -jnp.dot(upper_p, sep_one, preferred_element_type=jnp.float32),
        "row",
        scatter_dimension=0,
        tiled=True,
    ).astype(jnp.bfloat16)
    lower_c = lax.all_gather(take_rows(lower_two, col_two), "row", axis=1, tiled=True)
    upper_c = lax.all_gather(take_cols(upper_two, row_two), "col", axis=0, tiled=True)
    own_rows = col_index * share_one + jnp.arange(share_one, dtype=jnp.int32)
    chooser = (lower_spots[:, None] == own_rows[None, :]).astype(jnp.float32)
    carried = jnp.dot(inv_lower_one, corner_lower, preferred_element_type=jnp.float32)
    direct = jnp.dot(sep_two, lower_c, preferred_element_type=jnp.float32)
    shifted_part = jnp.dot(chooser, carried, precision=lax.Precision.HIGHEST)
    inv_lower_two = lax.psum_scatter(
        -(direct + shifted_part), "col", scatter_dimension=0, tiled=True
    ).astype(jnp.bfloat16)
    ancestor_cols = take_cols(inv_upper_one, upper_spots)
    direct = jnp.dot(upper_c, sep_two, preferred_element_type=jnp.float32)
    shifted_part = jnp.dot(corner_mine, ancestor_cols, preferred_element_type=jnp.float32)
    inv_upper_two = lax.psum_scatter(
        -(direct + shifted_part), "row", scatter_dimension=0, tiled=True
    ).astype(jnp.bfloat16)
    upper_slab = lax.dynamic_slice_in_dim(upper_p, col_index * share_one, share_one, 1)
    second_slab = lax.dynamic_slice_in_dim(upper_c, col_index * share_two, share_two, 1)
    first_part = jnp.dot(upper_slab, inv_lower_one, preferred_element_type=jnp.float32)
    cross = jnp.dot(ancestor_cols, lower_c, preferred_element_type=jnp.float32)
    second_part = jnp.dot(second_slab, inv_lower_two, preferred_element_type=jnp.float32) - highest(
        corner_mine, cross
    )
    extra_part = highest(corner_upper, highest(first_part, corner_lower))
    first_total, second_total = lax.psum((first_part, second_part + extra_part), ("row", "col"))
    inv_diag_one = diag_inv_one - first_total
    tail_term = highest(corner_upper, highest(diag_inv_one, corner_lower))
    inv_diag_two = diag_inv_two - (second_total - tail_term)
    return (inv_lower_one, inv_upper_one, inv_diag_one, inv_lower_two, inv_upper_two, inv_diag_two)


def solution(mesh):
    return jax.shard_map(
        on_device,
        mesh=mesh,
        in_specs=(
            P("row", "col"),
            P("col", "row"),
            P("col", "row"),
            P(),
            P(),
            P("col", "row"),
            P("col", "row"),
            P(),
            P(),
            P(),
            P(),
        ),
        out_specs=(
            P(("row", "col"), None),
            P("row", "col"),
            P(),
            P(("row", "col"), None),
            P("row", "col"),
            P(),
        ),
        check_vma=False,
    )
```

profile of v0, /device:TPU:0, one launch (start us, length us, event | category | flops | bytes accessed | tf_op | source)
XLA Modules:
  0.0 326.3 jit_solution(9898332100142515147)
XLA Ops:
  8.0 8.9 %gather_fusion = bf16[10,128,3072]{2,1,0:T(8,128)(2,1)} fusion(bf16[48,128,3072]{2,1,0:T(8,128)(2,1)} %bitcast.126, s32[1024]{0:T(1024)S(1)} %pad_clamp_fusion.4), kind=kCustom, calls=%fused_computation | custom fusion | bytes 15728680 | tf_op jit(solution)/shard_map/jit(_take)/gather | solution.py:19
  16.9 8.3 %copy.69 = bf16[160,8,24,128]{3,2,1,0:T(8,128)(2,1)} copy(bf16[160,8,24,128]{3,1,2,0:T(8,128)(2,1)} %bitcast.121) | data formatting | bytes 15728640
  25.4 8.6 %copy_select_fusion = bf16[1280,24,128]{2,0,1:T(8,128)(2,1)} fusion(bf16[1280,24,128]{2,1,0:T(8,128)(2,1)} %bitcast.122, pred[1280]{0:T(1024)(128)(4,1)S(1)} %broadcast_bitcast_fusion), kind=kLoop, calls=%fused_computation.9 | loop fusion | flops 3932160 | bytes 15729920 | tf_op jit(solution)/shard_map/jit(_take)/select_n | solution.py:19
  34.0 4.1 %gather_fusion.1 = bf16[5,1280,128]{2,1,0:T(8,128)(2,1)S(1)} fusion(bf16[1280,24,128]{2,0,1:T(8,128)(2,1)} %copy_select_fusion, s32[1024]{0:T(1024)S(1)} %pad_clamp_fusion.3), kind=kCustom, calls=%fused_computation.1 | custom fusion | bytes 3276820 | tf_op jit(solution)/shard_map/jit(_take)/gather | solution.py:24
  38.1 2.4 copy.42
  41.2 1.6 bitcast_select_fusion
  42.9 11.0 %all_gather.12 = bf16[640,256]{0,1:T(8,128)(2,1)S(1)} all-gather(bf16[640,64]{0,1:T(8,128)(2,1)S(1)} %bitcast_select_fusion.3), channel_id=1, replica_groups=mesh['row'=4,'col'=8] {'row'}, dimensions={1}, use_global_device_ids=true | all-gather | bytes 409600 | tf_op jit(solution)/shard_map/all_gather | solution.py:82
  53.8 1.8 convolution_negate_fusion
  56.4 17.9 %all_gather.13 = bf16[256,1280]{1,0:T(8,128)(2,1)S(1)} all-gather(bf16[32,1280]{1,0:T(8,128)(2,1)S(1)} %bitcast_select_fusion.2), channel_id=1, replica_groups=mesh['row'=4,'col'=8] {'col'}, dimensions={0}, use_global_device_ids=true | all-gather | bytes 737280 | tf_op jit(solution)/shard_map/all_gather | solution.py:83
  77.2 6.5 %gather_fusion.4 = bf16[8,128,3072]{2,1,0:T(8,128)(2,1)} fusion(bf16[48,128,3072]{2,1,0:T(8,128)(2,1)} %bitcast.127, s32[1024]{0:T(1024)S(1)} %pad_clamp_fusion.2), kind=kCustom, calls=%fused_computation.4 | custom fusion | bytes 12582944 | tf_op jit(solution)/shard_map/jit(_take)/gather | solution.py:19
  83.6 4.8 %copy.70 = bf16[128,8,24,128]{3,2,1,0:T(8,128)(2,1)S(1)} copy(bf16[128,8,24,128]{3,1,2,0:T(8,128)(2,1)} %bitcast.124) | data formatting | bytes 12582912
  88.5 4.2 %copy_select_fusion.1 = bf16[1024,24,128]{2,0,1:T(8,128)(2,1)} fusion(bf16[1024,24,128]{2,1,0:T(8,128)(2,1)S(1)} %bitcast.123, pred[1024]{0:T(1024)(128)(4,1)S(1)} %broadcast_bitcast_fusion.1), kind=kLoop, calls=%fused_computation.10 | loop fusion | flops 3145728 | bytes 12583936 | tf_op jit(solution)/shard_map/jit(_take)/select_n | solution.py:19
  92.7 3.6 %gather_fusion.5 = bf16[4,1024,128]{2,1,0:T(8,128)(2,1)S(1)} fusion(bf16[1024,24,128]{2,0,1:T(8,128)(2,1)} %copy_select_fusion.1, s32[1024]{0:T(1024)S(1)} %pad_clamp_fusion.1), kind=kCustom, calls=%fused_computation.5 | custom fusion | bytes 2097168 | tf_op jit(solution)/shard_map/jit(_take)/gather | solution.py:24
  98.6 9.4 %all_gather.14 = bf16[512,256]{0,1:T(8,128)(2,1)S(1)} all-gather(bf16[512,64]{0,1:T(8,128)(2,1)S(1)} %bitcast_select_fusion.6), channel_id=1, replica_groups=mesh['row'=4,'col'=8] {'row'}, dimensions={1}, use_global_device_ids=true | all-gather | bytes 327680 | tf_op jit(solution)/shard_map/all_gather | solution.py:96
  108.7 1.8 copy_bitcast_fusion
  112.4 1.6 fusion
  114.2 1.6 gather_fusion.7
  115.9 14.9 %all_gather.15 = bf16[256,1024]{1,0:T(8,128)(2,1)S(1)} all-gather(bf16[32,1024]{1,0:T(8,128)(2,1)S(1)} %bitcast_select_fusion.5), channel_id=1, replica_groups=mesh['row'=4,'col'=8] {'col'}, dimensions={0}, use_global_device_ids=true | all-gather | bytes 589824 | tf_op jit(solution)/shard_map/all_gather | solution.py:97
  137.7 16.5 %reduce-scatter.9.cloned.1.call-done = f32[128,256]{1,0:T(8,128)} async-done(((f32[1024,256]{1,0:T(8,128)}), f32[128,256]{1,0:T(8,128)}) %reduce-scatter.9.cloned.1.call-update) | async-done | bytes 131088 | tf_op jit(solution)/shard_map/reduce_scatter | solution.py:103
  156.5 1.9 fusion.4
  160.3 20.3 %reduce-scatter.11.cloned.1.call-done = f32[64,512]{1,0:T(8,128)} async-done(((f32[256,512]{1,0:T(8,128)}), f32[64,512]{1,0:T(8,128)}) %reduce-scatter.11.cloned.1.call-update) | async-done | bytes 131088 | tf_op jit(solution)/shard_map/reduce_scatter | solution.py:109
  182.2 133.7 %all-reduce.3.cloned.1.call-done = (f32[256,256]{1,0:T(8,128)}, f32[256,256]{1,0:T(8,128)}) async-done(((f32[256,256]{1,0:T(8,128)}, f32[256,256]{1,0:T(8,128)}), (f32[256,256]{1,0:T(8,128)}, f32[256,256]{1,0:T(8,128)})) %all-reduce.3.cloned.1.call-update) | async-done | bytes 524304 | tf_op jit(solution)/shard_map/psum | solution.py:120
  315.9 1.8 sub.40
  317.7 2.1 fusion.3
  (88 shorter events, 23.0 us)
Async XLA Ops:
  7.2 33.4 %copy-start = (bf16[3072,64]{0,1:T(8,128)(2,1)S(1)}, bf16[3072,64]{0,1:T(8,128)(2,1)}, u32[]{:S(2)}) copy-start(bf16[3072,64]{0,1:T(8,128)(2,1)} %param.12) | copy-start | bytes 1179652
  7.2 104.1 %reduce-scatter.5.cloned.1.call-start = ((), (), s32[]{:S(2)}) async-start(), calls=%async_computation.4 | async-start | bytes 1474560 | tf_op jit(solution)/shard_map/reduce_scatter | solution.py:84
  16.9 8.3 %copy-start.9 = (s32[40]{0:T(128)S(1)}, s32[40]{0:T(128)}, u32[]{:S(2)}) copy-start(s32[40]{0:T(128)} %param.15) | copy-start | bytes 484
  40.4 15.3 %copy-start.7 = (bf16[32,6144]{1,0:T(8,128)(2,1)S(1)}, bf16[32,6144]{1,0:T(8,128)(2,1)}, u32[]{:S(2)}) copy-start(bf16[32,6144]{1,0:T(8,128)(2,1)} %param.13) | copy-start | bytes 1179652
  53.8 22.3 %copy-start.10 = (s32[32]{0:T(128)S(1)}, s32[32]{0:T(128)}, u32[]{:S(2)}) copy-start(s32[32]{0:T(128)} %param.21) | copy-start | bytes 388
  55.7 75.1 %reduce-scatter.7.cloned.1.call-start = ((), (), s32[]{:S(2)}) async-start(), calls=%async_computation.5 | async-start | bytes 819200 | tf_op jit(solution)/shard_map/reduce_scatter | solution.py:90
  75.9 78.3 %reduce-scatter.9.cloned.1.call-start = ((), (), s32[]{:S(2)}) async-start(), calls=%async_computation.6 | async-start | bytes 1179648 | tf_op jit(solution)/shard_map/reduce_scatter | solution.py:103
  92.7 19.5 %copy-start.3 = (bf16[256,256]{1,0:T(8,128)(2,1)S(1)}, bf16[256,256]{1,0:T(8,128)(2,1)}, u32[]{:S(2)}) copy-start(bf16[256,256]{1,0:T(8,128)(2,1)} %param.18) | copy-start | bytes 393220
  112.3 1.8 copy-start.4
  114.1 205.7 %copy-start.1 = (bf16[3072,64]{0,1:T(8,128)(2,1)S(1)}, bf16[3072,64]{0,1:T(8,128)(2,1)}, u32[]{:S(2)}) copy-start(bf16[3072,64]{0,1:T(8,128)(2,1)} %param.12) | copy-start | bytes 1179652
  114.1 66.5 %reduce-scatter.11.cloned.1.call-start = ((), (), s32[]{:S(2)}) async-start(), calls=%async_computation.7 | async-start | bytes 655360 | tf_op jit(solution)/shard_map/reduce_scatter | solution.py:109
  132.2 0.6 copy-start.6
  133.7 25.9 %copy-start.5 = (f32[64,640]{1,0:T(8,128)S(1)}, f32[64,640]{1,0:T(8,128)}, u32[]{:S(2)}) copy-start(f32[64,640]{1,0:T(8,128)} %reduce-scatter.7.cloned.1.call-done) | copy-start | bytes 491524
  136.2 179.7 %all-reduce.3.cloned.1.call-start = ((), (), s32[]{:S(2)}) async-start(), calls=%async_computation.8 | async-start | bytes 1048576 | tf_op jit(solution)/shard_map/psum | solution.py:120
  137.4 21.0 %copy-start.2 = (f32[256,256]{1,0:T(8,128)}, f32[256,256]{1,0:T(8,128)S(1)}, u32[]{:S(2)}) copy-start(f32[256,256]{1,0:T(8,128)S(1)} %fusion.8) | copy-start | bytes 786436
  155.1 164.7 %copy-start.8 = (bf16[128,256]{1,0:T(8,128)(2,1)}, bf16[128,256]{1,0:T(8,128)(2,1)S(1)}, u32[]{:S(2)}) copy-start(bf16[128,256]{1,0:T(8,128)(2,1)S(1)} %convert_element_type.27) | copy-start | bytes 196612
Sparse Core Ops, SparseCore 0:
  55.8 34.1 reduce-scatter.4
  92.8 26.3 reduce-scatter.6
  121.5 32.5 reduce-scatter.8
  156.9 23.7 reduce-scatter.10
  186.5 129.3 all-reduce.2
where the time goes:
time: 327 us; the launch traced here: 326 us
  waiting for transfers between devices  171 us (52%)
  blocking collectives  53.1 us (16%)
  local copies, waits for them, and re-layouts  46.9 us (14%)
  other arithmetic  24.2 us (7%)
  matrix products  16.9 us (5%)
  between operations  14.1 us (4%)
    psum x1, waiting for transfers between devices, on_device(): lax.psum((first_part, second_part + extra_part), ('row', 'col'))  134 us
    reduce_scatter x1, waiting for transfers between devices, on_device(): lax.psum_scatter(-(direct + shifted_part), 'row', scatter_dimension=0, ti...  20.3 us
    all_gather x1, blocking collectives, on_device(): lax.all_gather(take_cols(upper_one, row_one), 'col', axis=0, tiled=True)  17.9 us
    reduce_scatter x1, waiting for transfers between devices, on_device(): lax.psum_scatter(-(direct + shifted_part), 'col', scatter_dimension=0, ti...  16.5 us
    gather x4, local copies, waits for them, and re-layouts, take_rows(): jnp.take(shaped, blocks, axis=0)  16.5 us
    all_gather x1, blocking collectives, on_device(): lax.all_gather(take_cols(upper_two, row_two), 'col', axis=0, tiled=True)  14.9 us
    unnamed x24, local copies, waits for them, and re-layouts  13.7 us
    gather x7, local copies, waits for them, and re-layouts, take_cols(): jnp.take(shaped, blocks, axis=1)  13.3 us
  transfers between devices with their start and end apart: 5, of which 3 were waited for; matrix products, arithmetic and copies ran while one was open for 14% of the time, Pallas kernels for 0%

commit v1 on v0

--- a/solution.py
+++ b/solution.py
@@ -80,7 +80,15 @@
     upper_spots = places(col_two, col_one)
     corner_mine = lax.dynamic_slice_in_dim(corner_upper, row_index * upper_rows, upper_rows, 1)
     lower_p = lax.all_gather(take_rows(lower_one, col_one), "row", axis=1, tiled=True)
-    upper_p = lax.all_gather(take_cols(upper_one, row_one), "col", axis=0, tiled=True)
+    x = take_cols(upper_one, row_one)
+    ways = lax.axis_size("col")
+    pieces = [x]
+    for far in range(1, ways):
+        pieces.append(
+            lax.ppermute(pieces[far - 1], "col", [(d, (d - 1) % ways) for d in range(ways)])
+        )
+    line = jnp.concatenate(pieces, axis=0)
+    upper_p = jnp.roll(line, lax.axis_index("col") * x.shape[0], axis=0)
     inv_lower_one = lax.psum_scatter(
         -jnp.dot(sep_one, lower_p, preferred_element_type=jnp.float32),
         "col",

time: 327 us -> 345 us (1.055)
  waiting for transfers between devices: 171 us -> 193 us
  starting transfers between devices: 0.39 us -> 21.8 us
  blocking collectives: 53.1 us -> 35 us
  matrix products: 16.9 us -> 12.7 us
    ppermute x0 -> x7, starting transfers between devices: none -> 21.6 us  [on_device(): lax.ppermute(pieces[far - 1], 'col', [(d, (d - 1) % ways) for d in range(...]
    all_gather x1 -> x0, blocking collectives: 17.9 us -> none  [on_device(): lax.all_gather(take_cols(upper_one, row_one), 'col', axis=0, tiled=True)]
    ppermute x0 -> x7, waiting for transfers between devices: none -> 12.3 us  [on_device(): lax.ppermute(pieces[far - 1], 'col', [(d, (d - 1) % ways) for d in range(...]
    reduce_scatter x1, waiting for transfers between devices: 16.5 us -> 24.2 us  [on_device(): lax.psum_scatter(-(direct + shifted_part), 'col', scatter_dimension=0, ti...]
    unnamed x24 -> x46, local copies, waits for them, and re-layouts: 13.7 us -> 14.6 us
  transfers between devices with their start and end apart: 5 -> 12, of which waited for: 3 -> 9; matrix products, arithmetic and copies ran while one was open for 14% -> 13% of each run, Pallas kernels for 0% -> 0%
where the time goes in v1:
time: 345 us
  waiting for transfers between devices  193 us (56%)
  local copies, waits for them, and re-layouts  44.2 us (13%)
  blocking collectives  35 us (10%)
  other arithmetic  23.7 us (7%)
  starting transfers between devices  21.8 us (6%)
  between operations  14.3 us (4%)
  matrix products  12.7 us (4%)
    psum x1, waiting for transfers between devices, on_device(): lax.psum((first_part, second_part + extra_part), ('row', 'col'))  134 us
    reduce_scatter x1, waiting for transfers between devices, on_device(): lax.psum_scatter(-(direct + shifted_part), 'col', scatter_dimension=0, ti...  24.2 us
    reduce_scatter x1, waiting for transfers between devices, on_device(): lax.psum_scatter(-(direct + shifted_part), 'row', scatter_dimension=0, ti...  22.6 us
    ppermute x7, starting transfers between devices, on_device(): lax.ppermute(pieces[far - 1], 'col', [(d, (d - 1) % ways) for d in range(...  21.6 us
    gather x4, local copies, waits for them, and re-layouts, take_rows(): jnp.take(shaped, blocks, axis=0)  16.6 us
    all_gather x1, blocking collectives, on_device(): lax.all_gather(take_cols(upper_two, row_two), 'col', axis=0, tiled=True)  14.8 us
    unnamed x46, local copies, waits for them, and re-layouts  14.6 us
    select_n x6, other arithmetic, take_rows(): jnp.take(shaped, blocks, axis=0)  12.4 us
  transfers between devices with their start and end apart: 12, of which 9 were waited for; matrix products, arithmetic and copies ran while one was open for 13% of the time, Pallas kernels for 0%

profile of v1, /device:TPU:0, one launch (start us, length us, event | category | flops | bytes accessed | tf_op | source)
XLA Modules:
  0.0 344.5 jit_solution(16373712340464076776)
XLA Ops:
  8.8 8.9 %gather_fusion = bf16[10,128,3072]{2,1,0:T(8,128)(2,1)} fusion(bf16[48,128,3072]{2,1,0:T(8,128)(2,1)} %bitcast.126, s32[1024]{0:T(1024)S(1)} %get-tuple-element.21), kind=kCustom, calls=%fused_computation | custom fusion | bytes 15728680 | tf_op jit(solution)/shard_map/jit(_take)/gather | solution.py:19
  17.7 5.2 %copy.69 = bf16[160,8,24,128]{3,2,1,0:T(8,128)(2,1)S(1)} copy(bf16[160,8,24,128]{3,1,2,0:T(8,128)(2,1)} %bitcast.121) | data formatting | bytes 15728640
  23.0 5.3 %copy_select_fusion = bf16[1280,24,128]{2,0,1:T(8,128)(2,1)} fusion(bf16[1280,24,128]{2,1,0:T(8,128)(2,1)S(1)} %bitcast.122, pred[1280]{0:T(1024)(128)(4,1)S(1)} %broadcast_bitcast_fusion), kind=kLoop, calls=%fused_computation.9 | loop fusion | flops 3932160 | bytes 15729920 | tf_op jit(solution)/shard_map/jit(_take)/select_n | solution.py:19
  28.2 4.1 %gather_fusion.1 = bf16[5,1280,128]{2,1,0:T(8,128)(2,1)S(1)} fusion(bf16[1280,24,128]{2,0,1:T(8,128)(2,1)} %copy_select_fusion, s32[1024]{0:T(1024)S(1)} %get-tuple-element.20), kind=kCustom, calls=%fused_computation.1 | custom fusion | bytes 3276820 | tf_op jit(solution)/shard_map/jit(_take)/gather | solution.py:24
  32.3 2.4 copy.42
  37.2 11.0 %all_gather.9 = bf16[640,256]{0,1:T(8,128)(2,1)S(1)} all-gather(bf16[640,64]{0,1:T(8,128)(2,1)S(1)} %bitcast_select_fusion.3), channel_id=1, replica_groups=mesh['row'=4,'col'=8] {'row'}, dimensions={1}, use_global_device_ids=true | all-gather | bytes 409600 | tf_op jit(solution)/shard_map/all_gather | solution.py:82
  53.8 6.5 %gather_fusion.4 = bf16[8,128,3072]{2,1,0:T(8,128)(2,1)} fusion(bf16[48,128,3072]{2,1,0:T(8,128)(2,1)} %bitcast.127, s32[1024]{0:T(1024)S(1)} %pad_clamp_fusion.2), kind=kCustom, calls=%fused_computation.4 | custom fusion | bytes 12582944 | tf_op jit(solution)/shard_map/jit(_take)/gather | solution.py:19
  60.3 7.4 %copy.70 = bf16[128,8,24,128]{3,2,1,0:T(8,128)(2,1)} copy(bf16[128,8,24,128]{3,1,2,0:T(8,128)(2,1)} %bitcast.124) | data formatting | bytes 12582912
  68.1 7.1 %copy_select_fusion.1 = bf16[1024,24,128]{2,0,1:T(8,128)(2,1)} fusion(bf16[1024,24,128]{2,1,0:T(8,128)(2,1)} %bitcast.123, pred[1024]{0:T(1024)(128)(4,1)S(1)} %broadcast_bitcast_fusion.1), kind=kLoop, calls=%fused_computation.10 | loop fusion | flops 3145728 | bytes 12583936 | tf_op jit(solution)/shard_map/jit(_take)/select_n | solution.py:19
  75.8 2.5 collective-permute-start.1
  78.3 2.1 collective-permute-done.1
  80.3 3.6 %collective-permute-start.2 = (bf16[32,1280]{1,0:T(8,128)(2,1)S(1)}, bf16[32,1280]{1,0:T(8,128)(2,1)S(1)}, u32[]{:S(2)}, u32[]{:S(2)}) collective-permute-start(bf16[32,1280]{1,0:T(8,128)(2,1)S(1)} %collective-permute-done.1), channel_id=1, source_target_pairs={{0,7},{1,0},{2,1},{3,2},{4,3},{5,4},{6,5},{7,6},{8,15},{9,8},{10,9... | collective-permute-start | bytes 245768 | tf_op jit(solution)/shard_map/ppermute | solution.py:88
  86.0 3.6 %collective-permute-start.3 = (bf16[32,1280]{1,0:T(8,128)(2,1)S(1)}, bf16[32,1280]{1,0:T(8,128)(2,1)S(1)}, u32[]{:S(2)}, u32[]{:S(2)}) collective-permute-start(bf16[32,1280]{1,0:T(8,128)(2,1)S(1)} %collective-permute-done.2), channel_id=1, source_target_pairs={{0,7},{1,0},{2,1},{3,2},{4,3},{5,4},{6,5},{7,6},{8,15},{9,8},{10,9... | collective-permute-start | bytes 245768 | tf_op jit(solution)/shard_map/ppermute | solution.py:88
  91.7 3.6 %collective-permute-start.4 = (bf16[32,1280]{1,0:T(8,128)(2,1)S(1)}, bf16[32,1280]{1,0:T(8,128)(2,1)S(1)}, u32[]{:S(2)}, u32[]{:S(2)}) collective-permute-start(bf16[32,1280]{1,0:T(8,128)(2,1)S(1)} %collective-permute-done.3), channel_id=1, source_target_pairs={{0,7},{1,0},{2,1},{3,2},{4,3},{5,4},{6,5},{7,6},{8,15},{9,8},{10,9... | collective-permute-start | bytes 245768 | tf_op jit(solution)/shard_map/ppermute | solution.py:88
  95.3 2.1 collective-permute-done.4
  97.3 3.6 %collective-permute-start.5 = (bf16[32,1280]{1,0:T(8,128)(2,1)S(1)}, bf16[32,1280]{1,0:T(8,128)(2,1)S(1)}, u32[]{:S(2)}, u32[]{:S(2)}) collective-permute-start(bf16[32,1280]{1,0:T(8,128)(2,1)S(1)} %collective-permute-done.4), channel_id=1, source_target_pairs={{0,7},{1,0},{2,1},{3,2},{4,3},{5,4},{6,5},{7,6},{8,15},{9,8},{10,9... | collective-permute-start | bytes 245768 | tf_op jit(solution)/shard_map/ppermute | solution.py:88
  100.9 2.1 collective-permute-done.5
  103.0 3.6 %collective-permute-start.6 = (bf16[32,1280]{1,0:T(8,128)(2,1)S(1)}, bf16[32,1280]{1,0:T(8,128)(2,1)S(1)}, u32[]{:S(2)}, u32[]{:S(2)}) collective-permute-start(bf16[32,1280]{1,0:T(8,128)(2,1)S(1)} %collective-permute-done.5), channel_id=1, source_target_pairs={{0,7},{1,0},{2,1},{3,2},{4,3},{5,4},{6,5},{7,6},{8,15},{9,8},{10,9... | collective-permute-start | bytes 245768 | tf_op jit(solution)/shard_map/ppermute | solution.py:88
  111.4 9.3 %all_gather.10 = bf16[512,256]{0,1:T(8,128)(2,1)S(1)} all-gather(bf16[512,64]{0,1:T(8,128)(2,1)S(1)} %bitcast_select_fusion.6), channel_id=1, replica_groups=mesh['row'=4,'col'=8] {'row'}, dimensions={1}, use_global_device_ids=true | all-gather | bytes 327680 | tf_op jit(solution)/shard_map/all_gather | solution.py:104
  120.6 3.6 %gather_fusion.5 = bf16[4,1024,128]{2,1,0:T(8,128)(2,1)S(1)} fusion(bf16[1024,24,128]{2,0,1:T(8,128)(2,1)} %copy_select_fusion.1, s32[1024]{0:T(1024)S(1)} %get-tuple-element.19), kind=kCustom, calls=%fused_computation.5 | custom fusion | bytes 2097168 | tf_op jit(solution)/shard_map/jit(_take)/gather | solution.py:24
  129.2 14.8 %all_gather.11 = bf16[256,1024]{1,0:T(8,128)(2,1)S(1)} all-gather(bf16[32,1024]{1,0:T(8,128)(2,1)S(1)} %bitcast_select_fusion.5), channel_id=1, replica_groups=mesh['row'=4,'col'=8] {'col'}, dimensions={0}, use_global_device_ids=true | all-gather | bytes 589824 | tf_op jit(solution)/shard_map/all_gather | solution.py:105
  148.9 24.2 %reduce-scatter.9.cloned.1.call-done = f32[128,256]{1,0:T(8,128)} async-done(((f32[1024,256]{1,0:T(8,128)}), f32[128,256]{1,0:T(8,128)}) %reduce-scatter.9.cloned.1.call-update) | async-done | bytes 131088 | tf_op jit(solution)/shard_map/reduce_scatter | solution.py:111
  176.5 22.6 %reduce-scatter.11.cloned.1.call-done = f32[64,512]{1,0:T(8,128)} async-done(((f32[256,512]{1,0:T(8,128)}), f32[64,512]{1,0:T(8,128)}) %reduce-scatter.11.cloned.1.call-update) | async-done | bytes 131088 | tf_op jit(solution)/shard_map/reduce_scatter | solution.py:117
  200.6 133.7 %all-reduce.3.cloned.1.call-done = (f32[256,256]{1,0:T(8,128)}, f32[256,256]{1,0:T(8,128)}) async-done(((f32[256,256]{1,0:T(8,128)}, f32[256,256]{1,0:T(8,128)}), (f32[256,256]{1,0:T(8,128)}, f32[256,256]{1,0:T(8,128)})) %all-reduce.3.cloned.1.call-update) | async-done | bytes 524304 | tf_op jit(solution)/shard_map/psum | solution.py:128
  (122 shorter events, 37.6 us)
Async XLA Ops:
  7.2 27.6 %copy-start = (bf16[3072,64]{0,1:T(8,128)(2,1)S(1)}, bf16[3072,64]{0,1:T(8,128)(2,1)}, u32[]{:S(2)}) copy-start(bf16[3072,64]{0,1:T(8,128)(2,1)} %param.12) | copy-start | bytes 1179652
  7.2 118.4 %reduce-scatter.5.cloned.1.call-start = ((), (), s32[]{:S(2)}) async-start(), calls=%async_computation.4 | async-start | bytes 1474560 | tf_op jit(solution)/shard_map/reduce_scatter | solution.py:92
  49.9 3.3 copy-start.14
  49.9 94.1 %reduce-scatter.7.cloned.1.call-start = ((), (), s32[]{:S(2)}) async-start(), calls=%async_computation.5 | async-start | bytes 819200 | tf_op jit(solution)/shard_map/reduce_scatter | solution.py:98
  52.2 23.5 %collective-permute-start = (bf16[32,1280]{1,0:T(8,128)(2,1)}, bf16[32,1280]{1,0:T(8,128)(2,1)S(1)}, u32[]{:S(2)}, u32[]{:S(2)}) collective-permute-start(bf16[32,1280]{1,0:T(8,128)(2,1)} %get-tuple-element.13), channel_id=1, source_target_pairs={{0,7},{1,0},{2,1},{3,2},{4,3},{5,4},{6,5},{7,6},{8,15},{9,8},{10,9... | collective-permute-start | bytes 245768 | tf_op jit(solution)/shard_map/ppermute | solution.py:88
  60.3 7.6 %copy-start.10 = (bf16[3072,64]{0,1:T(8,128)(2,1)S(1)}, bf16[3072,64]{0,1:T(8,128)(2,1)}, u32[]{:S(2)}) copy-start(bf16[3072,64]{0,1:T(8,128)(2,1)} %param.16) | copy-start | bytes 1179652
  75.8 4.6 %collective-permute-start.1 = (bf16[32,1280]{1,0:T(8,128)(2,1)S(1)}, bf16[32,1280]{1,0:T(8,128)(2,1)S(1)}, u32[]{:S(2)}, u32[]{:S(2)}) collective-permute-start(bf16[32,1280]{1,0:T(8,128)(2,1)S(1)} %collective-permute-done), channel_id=1, source_target_pairs={{0,7},{1,0},{2,1},{3,2},{4,3},{5,4},{6,5},{7,6},{8,15},{9,8},{10,9... | collective-permute-start | bytes 245768 | tf_op jit(solution)/shard_map/ppermute | solution.py:88
  80.3 5.7 %collective-permute-start.2 = (bf16[32,1280]{1,0:T(8,128)(2,1)S(1)}, bf16[32,1280]{1,0:T(8,128)(2,1)S(1)}, u32[]{:S(2)}, u32[]{:S(2)}) collective-permute-start(bf16[32,1280]{1,0:T(8,128)(2,1)S(1)} %collective-permute-done.1), channel_id=1, source_target_pairs={{0,7},{1,0},{2,1},{3,2},{4,3},{5,4},{6,5},{7,6},{8,15},{9,8},{10,9... | collective-permute-start | bytes 245768 | tf_op jit(solution)/shard_map/ppermute | solution.py:88
  86.0 5.7 %collective-permute-start.3 = (bf16[32,1280]{1,0:T(8,128)(2,1)S(1)}, bf16[32,1280]{1,0:T(8,128)(2,1)S(1)}, u32[]{:S(2)}, u32[]{:S(2)}) collective-permute-start(bf16[32,1280]{1,0:T(8,128)(2,1)S(1)} %collective-permute-done.2), channel_id=1, source_target_pairs={{0,7},{1,0},{2,1},{3,2},{4,3},{5,4},{6,5},{7,6},{8,15},{9,8},{10,9... | collective-permute-start | bytes 245768 | tf_op jit(solution)/shard_map/ppermute | solution.py:88
  91.7 5.7 %collective-permute-start.4 = (bf16[32,1280]{1,0:T(8,128)(2,1)S(1)}, bf16[32,1280]{1,0:T(8,128)(2,1)S(1)}, u32[]{:S(2)}, u32[]{:S(2)}) collective-permute-start(bf16[32,1280]{1,0:T(8,128)(2,1)S(1)} %collective-permute-done.3), channel_id=1, source_target_pairs={{0,7},{1,0},{2,1},{3,2},{4,3},{5,4},{6,5},{7,6},{8,15},{9,8},{10,9... | collective-permute-start | bytes 245768 | tf_op jit(solution)/shard_map/ppermute | solution.py:88
  97.3 5.7 %collective-permute-start.5 = (bf16[32,1280]{1,0:T(8,128)(2,1)S(1)}, bf16[32,1280]{1,0:T(8,128)(2,1)S(1)}, u32[]{:S(2)}, u32[]{:S(2)}) collective-permute-start(bf16[32,1280]{1,0:T(8,128)(2,1)S(1)} %collective-permute-done.4), channel_id=1, source_target_pairs={{0,7},{1,0},{2,1},{3,2},{4,3},{5,4},{6,5},{7,6},{8,15},{9,8},{10,9... | collective-permute-start | bytes 245768 | tf_op jit(solution)/shard_map/ppermute | solution.py:88
  103.0 5.7 %collective-permute-start.6 = (bf16[32,1280]{1,0:T(8,128)(2,1)S(1)}, bf16[32,1280]{1,0:T(8,128)(2,1)S(1)}, u32[]{:S(2)}, u32[]{:S(2)}) collective-permute-start(bf16[32,1280]{1,0:T(8,128)(2,1)S(1)} %collective-permute-done.5), channel_id=1, source_target_pairs={{0,7},{1,0},{2,1},{3,2},{4,3},{5,4},{6,5},{7,6},{8,15},{9,8},{10,9... | collective-permute-start | bytes 245768 | tf_op jit(solution)/shard_map/ppermute | solution.py:88
  111.3 61.7 %reduce-scatter.9.cloned.1.call-start = ((), (), s32[]{:S(2)}) async-start(), calls=%async_computation.6 | async-start | bytes 1179648 | tf_op jit(solution)/shard_map/reduce_scatter | solution.py:111
  126.5 20.9 %copy-start.6 = (bf16[160,256]{1,0:T(8,128)(2,1)}, bf16[160,256]{1,0:T(8,128)(2,1)S(1)}, u32[]{:S(2)}) copy-start(bf16[160,256]{1,0:T(8,128)(2,1)S(1)} %convert_element_type.24) | copy-start | bytes 245764
  126.7 1.7 copy-start.11
  128.4 17.4 %copy-start.4 = (bf16[256,256]{1,0:T(8,128)(2,1)S(1)}, bf16[256,256]{1,0:T(8,128)(2,1)}, u32[]{:S(2)}) copy-start(bf16[256,256]{1,0:T(8,128)(2,1)} %param.19) | copy-start | bytes 393220
  128.4 70.7 %reduce-scatter.11.cloned.1.call-start = ((), (), s32[]{:S(2)}) async-start(), calls=%async_computation.7 | async-start | bytes 655360 | tf_op jit(solution)/shard_map/reduce_scatter | solution.py:117
  147.3 187.0 %all-reduce.3.cloned.1.call-start = ((), (), s32[]{:S(2)}) async-start(), calls=%async_computation.8 | async-start | bytes 1048576 | tf_op jit(solution)/shard_map/psum | solution.py:128
  148.6 26.9 %copy-start.2 = (f32[256,256]{1,0:T(8,128)}, f32[256,256]{1,0:T(8,128)S(1)}, u32[]{:S(2)}) copy-start(f32[256,256]{1,0:T(8,128)S(1)} %fusion.9) | copy-start | bytes 786436
  148.9 26.6 %copy-start.5 = (f32[256,256]{1,0:T(8,128)S(1)}, f32[256,256]{1,0:T(8,128)}, u32[]{:S(2)}) copy-start(f32[256,256]{1,0:T(8,128)} %param.14) | copy-start | bytes 786436
  173.9 1.9 copy-start.12
  174.1 1.7 copy-start.7
  175.5 160.5 %copy-start.13 = (f32[256,256]{1,0:T(8,128)S(1)}, f32[256,256]{1,0:T(8,128)}, u32[]{:S(2)}) copy-start(f32[256,256]{1,0:T(8,128)} %param.20) | copy-start | bytes 786436
  175.5 162.5 %copy-start.1 = (bf16[3072,64]{0,1:T(8,128)(2,1)S(1)}, bf16[3072,64]{0,1:T(8,128)(2,1)}, u32[]{:S(2)}) copy-start(bf16[3072,64]{0,1:T(8,128)(2,1)} %param.12) | copy-start | bytes 1179652
  (3 other events, 4.1 us)
Sparse Core Ops, SparseCore 0:
  50.1 33.5 reduce-scatter.4
  111.4 26.6 reduce-scatter.6
  140.4 32.6 reduce-scatter.8
  175.7 23.2 reduce-scatter.10
  204.9 129.3 all-reduce.2
